TPU v7x, 32 devices: a whole 2x2x4 slice. The times are simulated.
32 devices in a mesh: samples: 8 (over z, y), snps: 4 (over x, core).
Axes of the slice: x: 2, y: 2, z: 4, core: 2. Of those that a mesh axis runs over, the one named last changes fastest.
Arguments:
- genotype: int32 [4096, 1536], P('samples', 'snps'), may hold values from 0 to 2
- mask: int32 [4096, 1536], P('samples', 'snps'), may hold values 0 or 1
Outputs:
- blocks: float32 [4096, 2560], P('samples', 'snps')
All inputs are finite; a program needn't handle non-finite values. No bound on the sum of `mask` on one device may be relied on, other than what follows from the above.
Results may differ from a plain program's by a relative error of at most 0.0014.
Values may be sent and summed in bfloat16 or wider, within the bound.
A program may use at most 128 MiB of HBM per device.

v0:
```python
import jax
import jax.numpy as jnp
from jax import lax
from jax.sharding import PartitionSpec as P


def passed_along(value, axis, steps):
    count = lax.axis_size(axis)
    pairs = [(source, (source + steps) % count) for source in range(count)]
    return lax.ppermute(value, axis, pairs)


def standardize(dosage, observed_mask, allele_sum, observed_sum):
    frequency = (allele_sum + 1.0) / (2.0 * observed_sum + 2.0)
    scaled = (
        observed_mask * (dosage - 2.0 * frequency) / jnp.sqrt(2.0 * frequency * (1.0 - frequency))
    )
    return scaled.astype(jnp.bfloat16)


def cross_block(own_rows, other_rows):
    return lax.dot_general(
        own_rows, other_rows, (((1,), (1,)), ((), ())), preferred_element_type=jnp.float32
    )


def place_block(target, block, offset):
    column = jnp.asarray(offset, jnp.int32) * block.shape[1]
    return lax.dynamic_update_slice(target, block, (jnp.int32(0), column))


def per_device(genotype, mask):
    dosage = genotype.astype(jnp.float32)
    observed_mask = mask.astype(jnp.float32)
    allele_sum, observed_sum = lax.psum(
        (jnp.sum(dosage * observed_mask, axis=0), jnp.sum(observed_mask, axis=0)), "samples"
    )
    standard = standardize(dosage, observed_mask, allele_sum, observed_sum)
    circle_size = lax.axis_size("samples")
    snp_parts = lax.axis_size("snps")
    block_rows = standard.shape[0]
    offsets = circle_size // 2 + 1
    snp_total = standard.shape[1] * snp_parts
    strip = jnp.zeros((block_rows, offsets * block_rows), jnp.float32)
    strip = place_block(strip, cross_block(standard, standard), 0)

    def advance(turn_index, carry):
        strip_now, holding = carry
        for second in range(2):
            holding = passed_along(holding, "samples", -1)
            strip_now = place_block(
                strip_now, cross_block(standard, holding), 2 * turn_index + second + 1
            )
        return (strip_now, holding)

    strip, holding_last = lax.fori_loop(0, circle_size // 4, advance, (strip, standard))
    summed = lax.psum_scatter(strip, "snps", scatter_dimension=1, tiled=True)
    return summed / snp_total


def solution(mesh):
    return jax.shard_map(
        per_device,
        mesh=mesh,
        in_specs=(P("samples", "snps"), P("samples", "snps")),
        out_specs=P("samples", "snps"),
        check_vma=False,
    )
```

profile of v0, /device:TPU:3, one launch (start us, length us, event | category | flops | bytes accessed | tf_op | source)
XLA Modules:
  0.0 137.8 jit_solution(3592213365028404441)
XLA Ops:
  6.5 0.0 reduce-scatter.2.cloned.1.call-start
  6.5 1.5 %multiply_reduce_fusion = (f32[384]{0:T(512)S(1)}, f32[384]{0:T(512)S(1)}) fusion(s32[512,384]{1,0:T(8,128)} %param.4, s32[512,384]{1,0:T(8,128)} %param.5), kind=kLoop, calls=%fused_computation.3 | loop fusion | flops 982272 | bytes 1575936 | tf_op jit(solution)/shard_map/reduce_sum | solution.py:36
  8.1 17.9 %all-reduce.1 = (f32[384]{0:T(512)S(1)}, f32[384]{0:T(512)S(1)}) all-reduce(f32[384]{0:T(512)S(1)} %get-tuple-element.117, f32[384]{0:T(512)S(1)} %get-tuple-element.116), channel_id=1, replica_groups=mesh['samples'=8,'snps'=4] {'samples'}, use_global_device_ids=true, to_apply=%region_3.0 | all-reduce | flops 768 | bytes 6144 | tf_op jit(solution)/shard_map/psum | solution.py:35
  26.0 1.5 %divide_convert_fusion = bf16[512,384]{1,0:T(8,128)(2,1)S(1)} fusion(s32[512,384]{1,0:T(8,128)} %param.4, s32[512,384]{1,0:T(8,128)} %param.5, f32[384]{0:T(512)S(1)} %multiply_sqrt_fusion, f32[384]{0:T(512)S(1)} %get-tuple-element.128), kind=kLoop, calls=%fused_computation.2 | loop fusion | flops 1179648 | bytes 1969152 | tf_op jit(solution)/shard_map/convert_element_type | solution.py:18
  27.6 0.5 fusion
  28.0 3.0 %dynamic_update_slice.23 = f32[512,2560]{1,0:T(8,128)} pad(f32[512,512]{1,0:T(8,128)S(1)} %fusion, f32[]{:T(128)} %constant.62.clone.1), padding=0_0x0_2048 | pad | bytes 6291460 | tf_op jit(solution)/shard_map/dynamic_update_slice | solution.py:29
  31.0 38.1 %while.17 = (s32[]{:T(128)}, f32[512,2560]{1,0:T(8,128)}, bf16[512,384]{1,0:T(8,128)(2,1)S(1)}, bf16[512,384]{1,0:T(8,128)(2,1)S(1)}, s32[]{:T(128)}, /*index=5*/s32[]{:T(128)}, s32[]{:T(128)}, s32[]{:T(128)}, s32[]{:T(128)}) while((s32[]{:T(128)}, f32[512,2560]{1,0:T(8,128)}, bf16[512,384]{1,0:T(8,128)(2,1)S(1)}, ...), condition=%wide.region_5.0_spmd, body=%wide.region_4.0_spmd.sunk | while | flops 402653184 | bytes 6816053 | solution.py:56
  31.0 0.0 collective-permute-start
  31.0 6.6 %collective-permute-done = bf16[512,384]{1,0:T(8,128)(2,1)S(1)} collective-permute-done((bf16[512,384]{1,0:T(8,128)(2,1)S(1)}, bf16[512,384]{1,0:T(8,128)(2,1)S(1)}, u32[]{:S(2)}, u32[]{:S(2)}) %collective-permute-start) | collective-permute-done | bytes 393248 | tf_op jit(solution)/shard_map/while/body/eval_jaxpr/ppermute | solution.py:10
  37.7 2.7 %collective-permute-start.1 = (bf16[512,384]{1,0:T(8,128)(2,1)S(1)}, bf16[512,384]{1,0:T(8,128)(2,1)S(1)}, u32[]{:S(2)}, u32[]{:S(2)}) collective-permute-start(bf16[512,384]{1,0:T(8,128)(2,1)S(1)} %collective-permute-done), channel_id=1, source_target_pairs={{0,28},{4,0},{8,4},{12,8},{16,12},{20,16},{24,20},{28,24},{1,29},{... | collective-permute-start | bytes 1179656 | tf_op jit(solution)/shard_map/while/body/eval_jaxpr/ppermute | solution.py:10
  40.4 1.5 %convolution_dynamic-update-slice_fusion.4 = f32[512,2560]{1,0:T(8,128)} fusion(f32[512,2560]{1,0:T(8,128)} %get-tuple-element.165, s32[]{:T(128)S(6)} %select_n.22, bf16[512,384]{1,0:T(8,128)(2,1)S(1)} %get-tuple-element.176, bf16[512,384]{1,0:T(8,128)(2,1)S(1)} %collective-permute-done), kind=kOutput, calls=%fused_computation.1.clone.1 | convolution fusion | flops 201326592 | bytes 1835012 | tf_op jit(solution)/shard_map/while/body/eval_jaxpr/dot_general | solution.py:22
  41.9 4.9 %collective-permute-done.1 = bf16[512,384]{1,0:T(8,128)(2,1)S(1)} collective-permute-done((bf16[512,384]{1,0:T(8,128)(2,1)S(1)}, bf16[512,384]{1,0:T(8,128)(2,1)S(1)}, u32[]{:S(2)}, u32[]{:S(2)}) %collective-permute-start.1) | collective-permute-done | bytes 393248 | tf_op jit(solution)/shard_map/while/body/eval_jaxpr/ppermute | solution.py:10
  46.8 1.5 %convolution_dynamic-update-slice_fusion.5 = f32[512,2560]{1,0:T(8,128)} fusion(f32[512,2560]{1,0:T(8,128)} %convolution_dynamic-update-slice_fusion.4, s32[]{:T(128)S(6)} %select_n.23, bf16[512,384]{1,0:T(8,128)(2,1)S(1)} %get-tuple-element.176, bf16[512,384]{1,0:T(8,128)(2,1)S(1)} %collective-permute-done.1), kind=kOutput, calls=%fused_computation.clone.1 | convolution fusion | flops 201326592 | bytes 1835012 | tf_op jit(solution)/shard_map/while/body/eval_jaxpr/dot_general | solution.py:22
  48.3 2.9 %collective-permute-start = (bf16[512,384]{1,0:T(8,128)(2,1)S(1)}, bf16[512,384]{1,0:T(8,128)(2,1)S(1)}, u32[]{:S(2)}, u32[]{:S(2)}) collective-permute-start(bf16[512,384]{1,0:T(8,128)(2,1)S(1)} %get-tuple-element.166), channel_id=1, source_target_pairs={{0,28},{4,0},{8,4},{12,8},{16,12},{20,16},{24,20},{28,24},{1,29},{... | collective-permute-start | bytes 1179656 | tf_op jit(solution)/shard_map/while/body/eval_jaxpr/ppermute | solution.py:10
  51.2 5.9 %collective-permute-done = bf16[512,384]{1,0:T(8,128)(2,1)S(1)} collective-permute-done((bf16[512,384]{1,0:T(8,128)(2,1)S(1)}, bf16[512,384]{1,0:T(8,128)(2,1)S(1)}, u32[]{:S(2)}, u32[]{:S(2)}) %collective-permute-start) | collective-permute-done | bytes 393248 | tf_op jit(solution)/shard_map/while/body/eval_jaxpr/ppermute | solution.py:10
  57.0 3.5 %collective-permute-start.1 = (bf16[512,384]{1,0:T(8,128)(2,1)S(1)}, bf16[512,384]{1,0:T(8,128)(2,1)S(1)}, u32[]{:S(2)}, u32[]{:S(2)}) collective-permute-start(bf16[512,384]{1,0:T(8,128)(2,1)S(1)} %collective-permute-done), channel_id=1, source_target_pairs={{0,28},{4,0},{8,4},{12,8},{16,12},{20,16},{24,20},{28,24},{1,29},{... | collective-permute-start | bytes 1179656 | tf_op jit(solution)/shard_map/while/body/eval_jaxpr/ppermute | solution.py:10
  60.5 1.5 %convolution_dynamic-update-slice_fusion.4 = f32[512,2560]{1,0:T(8,128)} fusion(f32[512,2560]{1,0:T(8,128)} %get-tuple-element.165, s32[]{:T(128)S(6)} %select_n.22, bf16[512,384]{1,0:T(8,128)(2,1)S(1)} %get-tuple-element.176, bf16[512,384]{1,0:T(8,128)(2,1)S(1)} %collective-permute-done), kind=kOutput, calls=%fused_computation.1.clone.1 | convolution fusion | flops 201326592 | bytes 1835012 | tf_op jit(solution)/shard_map/while/body/eval_jaxpr/dot_general | solution.py:22
  62.0 5.6 %collective-permute-done.1 = bf16[512,384]{1,0:T(8,128)(2,1)S(1)} collective-permute-done((bf16[512,384]{1,0:T(8,128)(2,1)S(1)}, bf16[512,384]{1,0:T(8,128)(2,1)S(1)}, u32[]{:S(2)}, u32[]{:S(2)}) %collective-permute-start.1) | collective-permute-done | bytes 393248 | tf_op jit(solution)/shard_map/while/body/eval_jaxpr/ppermute | solution.py:10
  67.6 1.5 %convolution_dynamic-update-slice_fusion.5 = f32[512,2560]{1,0:T(8,128)} fusion(f32[512,2560]{1,0:T(8,128)} %convolution_dynamic-update-slice_fusion.4, s32[]{:T(128)S(6)} %select_n.23, bf16[512,384]{1,0:T(8,128)(2,1)S(1)} %get-tuple-element.176, bf16[512,384]{1,0:T(8,128)(2,1)S(1)} %collective-permute-done.1), kind=kOutput, calls=%fused_computation.clone.1 | convolution fusion | flops 201326592 | bytes 1835012 | tf_op jit(solution)/shard_map/while/body/eval_jaxpr/dot_general | solution.py:22
  69.1 0.0 reduce-scatter.2.cloned.1.call-update
  69.1 59.3 %reduce-scatter.2.cloned.1.call-done = f32[512,640]{1,0:T(8,128)} async-done(((f32[512,2560]{1,0:T(8,128)}), f32[512,640]{1,0:T(8,128)}) %reduce-scatter.2.cloned.1.call-update) | async-done | bytes 1310736 | tf_op jit(solution)/shard_map/reduce_scatter | solution.py:57
  128.4 2.5 %broadcast_multiply_fusion = f32[512,640]{1,0:T(8,128)} fusion(f32[512,640]{1,0:T(8,128)} %reduce-scatter.2.cloned.1.call-done), kind=kLoop, calls=%fused_computation.5 | loop fusion | flops 327680 | bytes 2621440 | tf_op jit(solution)/shard_map/div | solution.py:58
  (3 shorter events, 0.1 us)
Async XLA Ops:
  6.5 121.9 %reduce-scatter.2.cloned.1.call-start = ((), (), s32[]{:S(2)}) async-start(), calls=%async_computation.1 | async-start | bytes 6553600 | tf_op jit(solution)/shard_map/reduce_scatter | solution.py:57
  31.0 6.6 %collective-permute-start = (bf16[512,384]{1,0:T(8,128)(2,1)S(1)}, bf16[512,384]{1,0:T(8,128)(2,1)S(1)}, u32[]{:S(2)}, u32[]{:S(2)}) collective-permute-start(bf16[512,384]{1,0:T(8,128)(2,1)S(1)} %get-tuple-element.166), channel_id=1, source_target_pairs={{0,28},{4,0},{8,4},{12,8},{16,12},{20,16},{24,20},{28,24},{1,29},{... | collective-permute-start | bytes 1179656 | tf_op jit(solution)/shard_map/while/body/eval_jaxpr/ppermute | solution.py:10
  37.7 9.1 %collective-permute-start.1 = (bf16[512,384]{1,0:T(8,128)(2,1)S(1)}, bf16[512,384]{1,0:T(8,128)(2,1)S(1)}, u32[]{:S(2)}, u32[]{:S(2)}) collective-permute-start(bf16[512,384]{1,0:T(8,128)(2,1)S(1)} %collective-permute-done), channel_id=1, source_target_pairs={{0,28},{4,0},{8,4},{12,8},{16,12},{20,16},{24,20},{28,24},{1,29},{... | collective-permute-start | bytes 1179656 | tf_op jit(solution)/shard_map/while/body/eval_jaxpr/ppermute | solution.py:10
  48.3 8.8 %collective-permute-start = (bf16[512,384]{1,0:T(8,128)(2,1)S(1)}, bf16[512,384]{1,0:T(8,128)(2,1)S(1)}, u32[]{:S(2)}, u32[]{:S(2)}) collective-permute-start(bf16[512,384]{1,0:T(8,128)(2,1)S(1)} %get-tuple-element.166), channel_id=1, source_target_pairs={{0,28},{4,0},{8,4},{12,8},{16,12},{20,16},{24,20},{28,24},{1,29},{... | collective-permute-start | bytes 1179656 | tf_op jit(solution)/shard_map/while/body/eval_jaxpr/ppermute | solution.py:10
  57.0 10.6 %collective-permute-start.1 = (bf16[512,384]{1,0:T(8,128)(2,1)S(1)}, bf16[512,384]{1,0:T(8,128)(2,1)S(1)}, u32[]{:S(2)}, u32[]{:S(2)}) collective-permute-start(bf16[512,384]{1,0:T(8,128)(2,1)S(1)} %collective-permute-done), channel_id=1, source_target_pairs={{0,28},{4,0},{8,4},{12,8},{16,12},{20,16},{24,20},{28,24},{1,29},{... | collective-permute-start | bytes 1179656 | tf_op jit(solution)/shard_map/while/body/eval_jaxpr/ppermute | solution.py:10
Sparse Core Ops, SparseCore 0:
  69.2 59.1 reduce-scatter.1
where the time goes:
time: 141 us; the launch traced here: 138 us
  waiting for transfers between devices  82.3 us (58%)
  blocking collectives  17.9 us (13%)
  between operations  13.4 us (10%)
  starting transfers between devices  9.07 us (6%)
  matrix products  6.47 us (5%)
  other arithmetic  5.56 us (4%)
  local copies, waits for them, and re-layouts  3.03 us (2%)
    reduce_scatter x1, waiting for transfers between devices, per_device(): summed = lax.psum_scatter(strip, 'snps', scatter_dimension=1, tiled=True)  59.3 us
    ppermute x4, waiting for transfers between devices, passed_along(): return lax.ppermute(value, axis, pairs)  23 us
    psum x1, blocking collectives, per_device(): lax.psum((jnp.sum(dosage * observed_mask, axis=0), jnp.sum(observed_mask,...  17.9 us
    ppermute x4, starting transfers between devices, passed_along(): return lax.ppermute(value, axis, pairs)  9.07 us
    dot_general x5, matrix products, cross_block(): lax.dot_general(own_rows, other_rows, (((1,), (1,)), ((), ())), preferred...  6.47 us
    dynamic_update_slice x1, local copies, waits for them, and re-layouts, place_block(): return lax.dynamic_update_slice(target, block, (jnp.int32(0), column))  2.98 us
  transfers between devices with their start and end apart: 5, of which 5 were waited for; matrix products, arithmetic and copies ran while one was open for 2% of the time, Pallas kernels for 0%

commit v1 on v0

v1 whole, which is shorter than its diff:
```python
import math

import jax
import jax.numpy as jnp
from jax import lax
from jax.sharding import PartitionSpec as P


def standardize(dosage, observed_mask, allele_sum, observed_sum):
    frequency = (allele_sum + 1.0) / (2.0 * observed_sum + 2.0)
    scaled = (
        observed_mask * (dosage - 2.0 * frequency) / jnp.sqrt(2.0 * frequency * (1.0 - frequency))
    )
    return scaled.astype(jnp.bfloat16)


def cross_block(own_rows, other_rows):
    return lax.dot_general(
        own_rows, other_rows, (((1,), (1,)), ((), ())), preferred_element_type=jnp.float32
    )


def rows_for_columns(full_rows, offsets):
    circle_size = lax.axis_size("samples")
    parts = lax.axis_size("snps")
    block_rows = full_rows.shape[0]
    width = offsets * block_rows // parts
    piece = math.gcd(block_rows, width)
    per_block = block_rows // piece
    per_part = width // piece
    part = lax.axis_index("snps")
    pieces = []
    for index in range(per_part):
        sub = (part * per_part + index) % per_block
        sent = lax.dynamic_slice_in_dim(full_rows, sub * piece, piece, axis=0)
        pairs = []
        for row in range(circle_size):
            for column in range(parts):
                ahead = (column * per_part + index) // per_block
                source = (row + ahead) % circle_size
                pairs.append((source * parts + column, row * parts + column))
        pieces.append(lax.ppermute(sent, ("samples", "snps"), pairs))
    return jnp.concatenate(pieces, axis=0)


def per_device(genotype, mask):
    dosage = genotype.astype(jnp.float32)
    observed_mask = mask.astype(jnp.float32)
    allele_sum, observed_sum = lax.psum(
        (jnp.sum(dosage * observed_mask, axis=0), jnp.sum(observed_mask, axis=0)), "samples"
    )
    standard = standardize(dosage, observed_mask, allele_sum, observed_sum)
    offsets = lax.axis_size("samples") // 2 + 1
    full_rows = lax.all_gather(standard, "snps", axis=1, tiled=True)
    others = rows_for_columns(full_rows, offsets)
    return cross_block(full_rows, others) / full_rows.shape[1]


def solution(mesh):
    return jax.shard_map(
        per_device,
        mesh=mesh,
        in_specs=(P("samples", "snps"), P("samples", "snps")),
        out_specs=P("samples", "snps"),
        check_vma=False,
    )
```

time: 141 us -> 140 us (level); the launches traced: 138 us -> 140 us
  starting transfers between devices: 9.07 us -> 15.8 us
  matrix products: 6.47 us -> 2.47 us
  waiting for transfers between devices: 82.3 us -> 86.1 us
  other arithmetic: 5.56 us -> 2.56 us
    reduce_scatter x1 -> x0, waiting for transfers between devices: 59.3 us -> none  [per_device(): summed = lax.psum_scatter(strip, 'snps', scatter_dimension=1, tiled=True)]
    ppermute x4 -> x5, waiting for transfers between devices: 23 us -> 66.1 us  [rows_for_columns(): pieces.append(lax.ppermute(sent, ('samples', 'snps'), pairs))]
    all_gather x0 -> x1, waiting for transfers between devices: none -> 20 us  [per_device(): full_rows = lax.all_gather(standard, 'snps', axis=1, tiled=True)]
    ppermute x4 -> x5, starting transfers between devices: 9.07 us -> 15.8 us  [rows_for_columns(): pieces.append(lax.ppermute(sent, ('samples', 'snps'), pairs))]
    dot_general x5 -> x1, matrix products: 6.47 us -> 2.47 us  [cross_block(): lax.dot_general(own_rows, other_rows, (((1,), (1,)), ((), ())), preferred...]
    dynamic_update_slice x1 -> x0, local copies, waits for them, and re-layouts: 2.98 us -> none  [place_block(): return lax.dynamic_update_slice(target, block, (jnp.int32(0), column))]
    div x1 -> x0, other arithmetic: 2.48 us -> none  [per_device(): return summed / snp_total]
    dynamic_slice x0 -> x1, local copies, waits for them, and re-layouts: none -> 1.6 us  [rows_for_columns(): sent = lax.dynamic_slice_in_dim(full_rows, sub * piece, piece, axis=0)]
  transfers between devices with their start and end apart: 5 -> 6, of which waited for: 5 -> 3; matrix products, arithmetic and copies ran while one was open for 2% -> 0% of each run, Pallas kernels for 0% -> 0%
where the time goes in v1:
time: 140 us
  waiting for transfers between devices  86.1 us (62%)
  blocking collectives  17.9 us (13%)
  starting transfers between devices  15.8 us (11%)
  between operations  13.6 us (10%)
  other arithmetic  2.56 us (2%)
  matrix products  2.47 us (2%)
  local copies, waits for them, and re-layouts  1.74 us (1%)
    ppermute x5, waiting for transfers between devices, rows_for_columns(): pieces.append(lax.ppermute(sent, ('samples', 'snps'), pairs))  66.1 us
    all_gather x1, waiting for transfers between devices, per_device(): full_rows = lax.all_gather(standard, 'snps', axis=1, tiled=True)  20 us
    psum x1, blocking collectives, per_device(): lax.psum((jnp.sum(dosage * observed_mask, axis=0), jnp.sum(observed_mask,...  17.9 us
    ppermute x5, starting transfers between devices, rows_for_columns(): pieces.append(lax.ppermute(sent, ('samples', 'snps'), pairs))  15.8 us
  transfers between devices with their start and end apart: 6, of which 3 were waited for; matrix products, arithmetic and copies ran while one was open for 0% of the time, Pallas kernels for 0%

profile of v1, /device:TPU:3, one launch (start us, length us, event | category | flops | bytes accessed | tf_op | source)
XLA Modules:
  0.0 140.2 jit_solution(2090311282719203152)
XLA Ops:
  6.5 0.0 copy-start.1
  6.5 0.0 copy-start
  6.5 0.0 all-gather.2.cloned.1.call-start
  6.5 1.6 %multiply_reduce_fusion = (f32[384]{0:T(512)S(1)}, f32[384]{0:T(512)S(1)}) fusion(s32[512,384]{1,0:T(8,128)} %param.2, s32[512,384]{1,0:T(8,128)} %param.3), kind=kLoop, calls=%fused_computation.2 | loop fusion | flops 982272 | bytes 1575936 | tf_op jit(solution)/shard_map/reduce_sum | solution.py:50
  8.2 17.9 %all-reduce = (f32[384]{0:T(512)S(1)}, f32[384]{0:T(512)S(1)}) all-reduce(f32[384]{0:T(512)S(1)} %get-tuple-element.6, f32[384]{0:T(512)S(1)} %get-tuple-element.5), channel_id=1, replica_groups=mesh['samples'=8,'snps'=4] {'samples'}, use_global_device_ids=true, to_apply=%region_3.0 | all-reduce | flops 768 | bytes 6144 | tf_op jit(solution)/shard_map/psum | solution.py:49
  26.1 0.0 copy-done.1
  26.1 0.0 copy-done
  26.1 0.9 divide_convert_fusion
  27.0 0.0 all-gather.2.cloned.1.call-update
  27.1 20.0 %all-gather.2.cloned.1.call-done = bf16[512,1536]{1,0:T(8,128)(2,1)} async-done(((bf16[512,384]{1,0:T(8,128)(2,1)}), bf16[512,1536]{1,0:T(8,128)(2,1)}) %all-gather.2.cloned.1.call-update) | async-done | bytes 1572880 | tf_op jit(solution)/shard_map/all_gather | solution.py:54
  47.1 1.6 %constant_dynamic-slice_fusion = (bf16[128,1536]{1,0:T(8,128)(2,1)S(1)}, bf16[128,1536]{1,0:T(8,128)(2,1)S(1)}, bf16[128,1536]{1,0:T(8,128)(2,1)S(1)}, bf16[128,1536]{1,0:T(8,128)(2,1)S(1)}, bf16[128,1536]{1,0:T(8,128)(2,1)S(1)}) fusion(bf16[512,1536]{1,0:T(8,128)(2,1)} %all-gather.2.cloned.1.call-done, s32[]{:T(128)S(6)} %select_n.47, s32[]{:T(128)S(6)} %select_n.45, ...), kind=kLoop, calls=%fused_computation.11 | loop fusion | bytes 3932180 | tf_op jit(solution)/shard_map/dynamic_slice | solution.py:35
  48.7 5.2 %collective-permute-start = (bf16[128,1536]{1,0:T(8,128)(2,1)S(1)}, bf16[128,1536]{1,0:T(8,128)(2,1)S(1)}, u32[]{:S(2)}, u32[]{:S(2)}) collective-permute-start(bf16[128,1536]{1,0:T(8,128)(2,1)S(1)} %get-tuple-element.15), channel_id=1, source_target_pairs={{0,0},{5,1},{10,2},{15,3},{4,4},{9,5},{14,6},{19,7},{8,8},{13,9},{... | collective-permute-start | bytes 1179656 | tf_op jit(solution)/shard_map/ppermute | solution.py:42
  53.9 2.1 %collective-permute-start.1 = (bf16[128,1536]{1,0:T(8,128)(2,1)S(1)}, bf16[128,1536]{1,0:T(8,128)(2,1)S(1)}, u32[]{:S(2)}, u32[]{:S(2)}) collective-permute-start(bf16[128,1536]{1,0:T(8,128)(2,1)S(1)} %get-tuple-element.14), channel_id=1, source_target_pairs={{0,0},{5,1},{10,2},{19,3},{4,4},{9,5},{14,6},{23,7},{8,8},{13,9},{... | collective-permute-start | bytes 1179656 | tf_op jit(solution)/shard_map/ppermute | solution.py:42
  56.0 2.2 %collective-permute-start.4 = (bf16[128,1536]{1,0:T(8,128)(2,1)S(1)}, bf16[128,1536]{1,0:T(8,128)(2,1)S(1)}, u32[]{:S(2)}, u32[]{:S(2)}) collective-permute-start(bf16[128,1536]{1,0:T(8,128)(2,1)S(1)} %get-tuple-element.11), channel_id=1, source_target_pairs={{4,0},{9,1},{14,2},{19,3},{8,4},{13,5},{18,6},{23,7},{12,8},{17,9}... | collective-permute-start | bytes 1179656 | tf_op jit(solution)/shard_map/ppermute | solution.py:42
  58.2 2.1 %collective-permute-start.3 = (bf16[128,1536]{1,0:T(8,128)(2,1)S(1)}, bf16[128,1536]{1,0:T(8,128)(2,1)S(1)}, u32[]{:S(2)}, u32[]{:S(2)}) collective-permute-start(bf16[128,1536]{1,0:T(8,128)(2,1)S(1)} %get-tuple-element.12), channel_id=1, source_target_pairs={{0,0},{9,1},{14,2},{19,3},{4,4},{13,5},{18,6},{23,7},{8,8},{17,9},... | collective-permute-start | bytes 1179656 | tf_op jit(solution)/shard_map/ppermute | solution.py:42
  60.3 0.0 copy-start.2
  60.3 4.2 %collective-permute-start.2 = (bf16[128,1536]{1,0:T(8,128)(2,1)S(1)}, bf16[128,1536]{1,0:T(8,128)(2,1)S(1)}, u32[]{:S(2)}, u32[]{:S(2)}) collective-permute-start(bf16[128,1536]{1,0:T(8,128)(2,1)S(1)} %get-tuple-element.13), channel_id=1, source_target_pairs={{0,0},{5,1},{14,2},{19,3},{4,4},{9,5},{18,6},{23,7},{8,8},{13,9},{... | collective-permute-start | bytes 1179656 | tf_op jit(solution)/shard_map/ppermute | solution.py:42
  64.5 0.0 collective-permute-done
  64.6 41.0 %collective-permute-done.1 = bf16[128,1536]{1,0:T(8,128)(2,1)S(1)} collective-permute-done((bf16[128,1536]{1,0:T(8,128)(2,1)S(1)}, bf16[128,1536]{1,0:T(8,128)(2,1)S(1)}, u32[]{:S(2)}, u32[]{:S(2)}) %collective-permute-start.1) | collective-permute-done | bytes 393248 | tf_op jit(solution)/shard_map/ppermute | solution.py:42
  105.6 25.1 %collective-permute-done.2 = bf16[128,1536]{1,0:T(8,128)(2,1)S(1)} collective-permute-done((bf16[128,1536]{1,0:T(8,128)(2,1)S(1)}, bf16[128,1536]{1,0:T(8,128)(2,1)S(1)}, u32[]{:S(2)}, u32[]{:S(2)}) %collective-permute-start.2) | collective-permute-done | bytes 393248 | tf_op jit(solution)/shard_map/ppermute | solution.py:42
  130.7 0.0 collective-permute-done.3
  130.8 0.0 collective-permute-done.4
  130.8 0.0 copy-done.2
  130.8 2.5 %convolution_multiply_fusion = f32[512,640]{1,0:T(8,128)} fusion(bf16[512,1536]{1,0:T(8,128)(2,1)S(1)} %copy-done.2, bf16[640,1536]{1,0:T(8,128)(2,1)S(1)} %constant_dynamic-update-slice_fusion), kind=kOutput, calls=%fused_computation | convolution fusion | flops 1006960640 | bytes 4849664 | tf_op jit(solution)/shard_map/dot_general | solution.py:18
  (7 shorter events, 0.2 us)
Async XLA Ops:
  6.5 19.6 %copy-start.1 = (s32[512,384]{1,0:T(8,128)S(1)}, s32[512,384]{1,0:T(8,128)}, u32[]{:S(2)}) copy-start(s32[512,384]{1,0:T(8,128)} %param.3) | copy-start | bytes 2359300
  6.5 19.6 %copy-start = (s32[512,384]{1,0:T(8,128)S(1)}, s32[512,384]{1,0:T(8,128)}, u32[]{:S(2)}) copy-start(s32[512,384]{1,0:T(8,128)} %param.2) | copy-start | bytes 2359300
  6.5 40.6 %all-gather.2.cloned.1.call-start = ((), (), s32[]{:S(2)}) async-start(), calls=%async_computation | async-start | bytes 1966080 | tf_op jit(solution)/shard_map/all_gather | solution.py:54
  48.7 15.8 %collective-permute-start = (bf16[128,1536]{1,0:T(8,128)(2,1)S(1)}, bf16[128,1536]{1,0:T(8,128)(2,1)S(1)}, u32[]{:S(2)}, u32[]{:S(2)}) collective-permute-start(bf16[128,1536]{1,0:T(8,128)(2,1)S(1)} %get-tuple-element.15), channel_id=1, source_target_pairs={{0,0},{5,1},{10,2},{15,3},{4,4},{9,5},{14,6},{19,7},{8,8},{13,9},{... | collective-permute-start | bytes 1179656 | tf_op jit(solution)/shard_map/ppermute | solution.py:42
  53.9 51.7 %collective-permute-start.1 = (bf16[128,1536]{1,0:T(8,128)(2,1)S(1)}, bf16[128,1536]{1,0:T(8,128)(2,1)S(1)}, u32[]{:S(2)}, u32[]{:S(2)}) collective-permute-start(bf16[128,1536]{1,0:T(8,128)(2,1)S(1)} %get-tuple-element.14), channel_id=1, source_target_pairs={{0,0},{5,1},{10,2},{19,3},{4,4},{9,5},{14,6},{23,7},{8,8},{13,9},{... | collective-permute-start | bytes 1179656 | tf_op jit(solution)/shard_map/ppermute | solution.py:42
  56.0 74.8 %collective-permute-start.4 = (bf16[128,1536]{1,0:T(8,128)(2,1)S(1)}, bf16[128,1536]{1,0:T(8,128)(2,1)S(1)}, u32[]{:S(2)}, u32[]{:S(2)}) collective-permute-start(bf16[128,1536]{1,0:T(8,128)(2,1)S(1)} %get-tuple-element.11), channel_id=1, source_target_pairs={{4,0},{9,1},{14,2},{19,3},{8,4},{13,5},{18,6},{23,7},{12,8},{17,9}... | collective-permute-start | bytes 1179656 | tf_op jit(solution)/shard_map/ppermute | solution.py:42
  58.2 72.6 %collective-permute-start.3 = (bf16[128,1536]{1,0:T(8,128)(2,1)S(1)}, bf16[128,1536]{1,0:T(8,128)(2,1)S(1)}, u32[]{:S(2)}, u32[]{:S(2)}) collective-permute-start(bf16[128,1536]{1,0:T(8,128)(2,1)S(1)} %get-tuple-element.12), channel_id=1, source_target_pairs={{0,0},{9,1},{14,2},{19,3},{4,4},{13,5},{18,6},{23,7},{8,8},{17,9},... | collective-permute-start | bytes 1179656 | tf_op jit(solution)/shard_map/ppermute | solution.py:42
  60.3 70.5 %copy-start.2 = (bf16[512,1536]{1,0:T(8,128)(2,1)S(1)}, bf16[512,1536]{1,0:T(8,128)(2,1)}, u32[]{:S(2)}) copy-start(bf16[512,1536]{1,0:T(8,128)(2,1)} %all-gather.2.cloned.1.call-done) | copy-start | bytes 4718596
  60.3 70.4 %collective-permute-start.2 = (bf16[128,1536]{1,0:T(8,128)(2,1)S(1)}, bf16[128,1536]{1,0:T(8,128)(2,1)S(1)}, u32[]{:S(2)}, u32[]{:S(2)}) collective-permute-start(bf16[128,1536]{1,0:T(8,128)(2,1)S(1)} %get-tuple-element.13), channel_id=1, source_target_pairs={{0,0},{5,1},{14,2},{19,3},{4,4},{9,5},{18,6},{23,7},{8,8},{13,9},{... | collective-permute-start | bytes 1179656 | tf_op jit(solution)/shard_map/ppermute | solution.py:42
Sparse Core Ops, SparseCore 0:
  27.2 19.8 all-gather.1
